TPU v7x, 256 devices: a whole 4x4x8 slice. The times are simulated.
256 devices in a mesh: tm: 16 (over z, core), row: 16 (over x, y).
Axes of the slice: x: 4, y: 4, z: 8, core: 2. Of those that a mesh axis runs over, the one named last changes fastest.
Arguments:
- prior_ensemble: float32 [128, 128, 4096], P('tm', None, 'row'), may hold values from -6 to 6
- observation_data: float32 [128, 8192], P('tm', 'row'), may hold values from -24 to 24
- inverse_error_spread: float32 [8192], P('row'), may hold values from 0.024902152 to 0.24902152
- anomaly_inflation: float32 [128], P('tm'), may hold values from 1.1 to 1.4
- nonzero_tiles: float32 [64, 8, 128, 128], P('row'), may hold values from -0.1875 to 0.1875
- nonzero_tile_targets: int32 [64, 8], P('row'), may hold values from 0 to 31, as said below
Outputs:
- smoothed_ensemble: float32 [128, 128, 4096], P('tm', None, 'row')
- filtered_ensemble: float32 [128, 128, 4096], P('tm', None, 'row')
Inputs may be any that keep to these rules, and one draw needn't show every extreme that they name: `nonzero_tile_targets`: in each block row the 8 block columns are distinct.
All inputs are finite; a program needn't handle non-finite values. Where the computation divides by a largest or mean magnitude, that divisor is 1e-20 or more.
Results may differ from a plain program's by a relative error of at most 0.0003.
Values sent between devices are 32-bit elements; how exact they have to be, the bound alone decides.
A program may use at most 64 MiB of HBM per device.

v0:
```python
import jax
import jax.numpy as jnp
from jax import lax
from jax.sharding import PartitionSpec as P

NS_ITERS = 8
exact_product = lax.Precision.HIGHEST


def passed_along(shard, axis, by):
    length = lax.axis_size(axis)
    pairs = [(i, i + by) for i in range(length) if 0 <= i + by < length]
    return lax.ppermute(shard, axis, pairs)


def ensemble_transforms(info_matrix, info_vector, anomaly_inflation):
    ensemble_entries = info_matrix.shape[-1]
    identity = jnp.eye(ensemble_entries, dtype=jnp.float32)
    row_bound = jnp.max(jnp.sum(jnp.abs(info_matrix), axis=2), axis=1)
    scaled = info_matrix / row_bound[:, None, None]
    root_iter = scaled
    inv_iter = jnp.broadcast_to(identity, scaled.shape)
    for _ in range(NS_ITERS):
        update = 1.5 * identity - 0.5 * jnp.matmul(inv_iter, root_iter, precision=exact_product)
        root_iter = jnp.matmul(root_iter, update, precision=exact_product)
        inv_iter = jnp.matmul(update, inv_iter, precision=exact_product)
    inverse_root = inv_iter / jnp.sqrt(row_bound)[:, None, None]
    half_weights = jnp.einsum("tab,tb->ta", inverse_root, info_vector, precision=exact_product)
    mean_weights = jnp.einsum("tab,tb->ta", inverse_root, half_weights, precision=exact_product)
    spread_norm = float(ensemble_entries - 1) ** 0.5
    mixing = (
        mean_weights[:, :, None] / spread_norm + anomaly_inflation[:, None, None] * inverse_root
    )
    mixing = mixing - jnp.mean(mixing, axis=1, keepdims=True)
    return mixing + 1.0 / ensemble_entries


def local(
    prior_ensemble,
    observation_data,
    inverse_error_spread,
    anomaly_inflation,
    nonzero_tiles,
    nonzero_tile_targets,
):
    ensemble_entries = prior_ensemble.shape[1]
    block_size = nonzero_tiles.shape[2]
    local_rows = nonzero_tiles.shape[0] * block_size

    def observe_single_time(ensemble_shard):
        whole = lax.all_gather(ensemble_shard, "row", axis=1, tiled=True)
        column_count = whole.shape[1] // block_size
        picked = whole.reshape(ensemble_entries, column_count, block_size)[:, nonzero_tile_targets]
        result = jnp.einsum("mbkj,bkij->mbi", picked, nonzero_tiles, precision=exact_product)
        return result.reshape(ensemble_entries, local_rows)

    predicted_observations = lax.map(observe_single_time, prior_ensemble)
    obs_mean = jnp.mean(predicted_observations, axis=1)
    whitened = (
        (predicted_observations - obs_mean[:, None, :])
        * inverse_error_spread
        / float(ensemble_entries - 1) ** 0.5
    )
    innovation = (observation_data - obs_mean) * inverse_error_spread
    part_matrix = jnp.einsum("tmo,tno->tmn", whitened, whitened, precision=exact_product)
    part_vector = jnp.einsum("tmo,to->tm", whitened, innovation, precision=exact_product)
    info_matrix, info_vector = lax.psum((part_matrix, part_vector), "row")
    identity = jnp.eye(ensemble_entries, dtype=jnp.float32)
    info_matrix = info_matrix + identity
    ensemble_weight_factors = ensemble_transforms(info_matrix, info_vector, anomaly_inflation)
    filtered_ensemble = jnp.einsum(
        "fjn,fjt->fnt", ensemble_weight_factors, prior_ensemble, precision=exact_product
    )

    def backward(running, transform):
        product = jnp.matmul(transform, running, precision=exact_product)
        return (product, product)

    _, local_trailing_sum = lax.scan(backward, identity, ensemble_weight_factors, reverse=True)
    shard_product = local_trailing_sum[0]
    final_index = lax.axis_size("tm") - 1
    position = lax.axis_index("tm")

    def one_hop(turn_index, current):
        outgoing = jnp.matmul(shard_product, current, precision=exact_product)
        received = passed_along(outgoing, "tm", -1)
        return jnp.where(position == final_index, identity, received)

    trailing_sum_end = lax.fori_loop(0, final_index, one_hop, identity)
    suffix_product = jnp.einsum(
        "jmk,kl->jml", local_trailing_sum, trailing_sum_end, precision=exact_product
    )
    smoothed_ensemble = jnp.einsum(
        "fjn,fjt->fnt", suffix_product, prior_ensemble, precision=exact_product
    )
    return (smoothed_ensemble, filtered_ensemble)


def solution(mesh):
    placed = (
        P("tm", None, "row"),
        P("tm", "row"),
        P("row"),
        P("tm"),
        P("row", None, None, None),
        P("row", None),
    )
    return jax.shard_map(
        local,
        mesh=mesh,
        in_specs=placed,
        out_specs=(P("tm", None, "row"), P("tm", None, "row")),
        check_vma=False,
    )
```

profile of v0, /device:TPU:97, one launch (start us, length us, event | category | flops | bytes accessed | tf_op | source)
XLA Modules:
  0.0 752.3 jit_solution(10505249584035878029)
XLA Ops:
  8.0 500.9 %while.39 = (s32[]{:T(128)}, f32[8,128,512]{1,2,0:T(8,128)}, f32[8,128,256]{2,1,0:T(8,128)}, s32[4,8]{1,0:T(4,128)}, f32[4,8,128,128]{3,2,1,0:T(8,128)}, /*index=5*/s32[]{:T(128)}) while((s32[]{:T(128)}, f32[8,128,512]{1,2,0:T(8,128)}, f32[8,128,256]{2,1,0:T(8,128)}, s32[4,8]{1,0:T(4,128)}, f32[4,8,128,128]{3,2,1,0:T(8,128)}, ...), condition=%wide.region_1.2_spmd, body=%wide.region_0.1_spmd.sunk | while | flops 805307520 | bytes 20583292 | solution.py:57
  10.6 52.6 %all-gather.5.cloned.1.call-done = f32[1,128,4096]{1,2,0:T(8,128)} async-done(((f32[1,128,256]{1,2,0:T(8,128)}), f32[1,128,4096]{1,2,0:T(8,128)}) %all-gather.5.cloned.1.call-update) | async-done | bytes 2097168 | tf_op jit(solution)/shard_map/while/body/eval_jaxpr/all_gather | solution.py:51
  65.1 2.0 gather_fusion
  67.1 4.3 fusion.116
  74.7 51.0 %all-gather.5.cloned.1.call-done = f32[1,128,4096]{1,2,0:T(8,128)} async-done(((f32[1,128,256]{1,2,0:T(8,128)}), f32[1,128,4096]{1,2,0:T(8,128)}) %all-gather.5.cloned.1.call-update) | async-done | bytes 2097168 | tf_op jit(solution)/shard_map/while/body/eval_jaxpr/all_gather | solution.py:51
  127.6 2.0 gather_fusion
  129.6 4.3 fusion.116
  137.2 51.0 %all-gather.5.cloned.1.call-done = f32[1,128,4096]{1,2,0:T(8,128)} async-done(((f32[1,128,256]{1,2,0:T(8,128)}), f32[1,128,4096]{1,2,0:T(8,128)}) %all-gather.5.cloned.1.call-update) | async-done | bytes 2097168 | tf_op jit(solution)/shard_map/while/body/eval_jaxpr/all_gather | solution.py:51
  190.1 2.0 gather_fusion
  192.1 4.3 fusion.116
  199.7 50.7 %all-gather.5.cloned.1.call-done = f32[1,128,4096]{1,2,0:T(8,128)} async-done(((f32[1,128,256]{1,2,0:T(8,128)}), f32[1,128,4096]{1,2,0:T(8,128)}) %all-gather.5.cloned.1.call-update) | async-done | bytes 2097168 | tf_op jit(solution)/shard_map/while/body/eval_jaxpr/all_gather | solution.py:51
  252.3 2.0 gather_fusion
  254.3 4.3 fusion.116
  261.9 50.7 %all-gather.5.cloned.1.call-done = f32[1,128,4096]{1,2,0:T(8,128)} async-done(((f32[1,128,256]{1,2,0:T(8,128)}), f32[1,128,4096]{1,2,0:T(8,128)}) %all-gather.5.cloned.1.call-update) | async-done | bytes 2097168 | tf_op jit(solution)/shard_map/while/body/eval_jaxpr/all_gather | solution.py:51
  314.5 2.0 gather_fusion
  316.5 4.3 fusion.116
  324.1 50.7 %all-gather.5.cloned.1.call-done = f32[1,128,4096]{1,2,0:T(8,128)} async-done(((f32[1,128,256]{1,2,0:T(8,128)}), f32[1,128,4096]{1,2,0:T(8,128)}) %all-gather.5.cloned.1.call-update) | async-done | bytes 2097168 | tf_op jit(solution)/shard_map/while/body/eval_jaxpr/all_gather | solution.py:51
  376.7 2.0 gather_fusion
  378.7 4.3 fusion.116
  386.3 51.0 %all-gather.5.cloned.1.call-done = f32[1,128,4096]{1,2,0:T(8,128)} async-done(((f32[1,128,256]{1,2,0:T(8,128)}), f32[1,128,4096]{1,2,0:T(8,128)}) %all-gather.5.cloned.1.call-update) | async-done | bytes 2097168 | tf_op jit(solution)/shard_map/while/body/eval_jaxpr/all_gather | solution.py:51
  439.3 2.0 gather_fusion
  441.3 4.3 fusion.116
  448.8 51.0 %all-gather.5.cloned.1.call-done = f32[1,128,4096]{1,2,0:T(8,128)} async-done(((f32[1,128,256]{1,2,0:T(8,128)}), f32[1,128,4096]{1,2,0:T(8,128)}) %all-gather.5.cloned.1.call-update) | async-done | bytes 2097168 | tf_op jit(solution)/shard_map/while/body/eval_jaxpr/all_gather | solution.py:51
  501.8 2.0 gather_fusion
  503.8 4.3 fusion.116
  508.9 2.3 reduce_sum.27
  511.3 5.6 fusion.7
  518.5 31.1 %psum.15 = f32[8,128]{1,0:T(8,128)S(1)} all-reduce(f32[8,128]{1,0:T(8,128)S(1)} %bitcast.123), channel_id=1, replica_groups=mesh['tm'=16,'row'=16] {'row'}, use_global_device_ids=true, to_apply=%region_6.7 | all-reduce | flops 1024 | bytes 8192 | tf_op jit(solution)/shard_map/psum | solution.py:67
  549.6 60.8 %all-reduce.2.cloned.1.call-done = f32[8,128,128]{2,1,0:T(8,128)} async-done(((f32[8,128,128]{2,1,0:T(8,128)}), f32[8,128,128]{2,1,0:T(8,128)}) %all-reduce.2.cloned.1.call-update) | async-done | bytes 524304 | tf_op jit(solution)/shard_map/psum | solution.py:67
  630.6 2.0 fusion.50
  634.7 107.5 %while.41 = (s32[]{:T(128)}, f32[128,128]{1,0:T(8,128)S(1)}, pred[]{:T(512)}, f32[128,128]{1,0:T(8,128)S(1)}, s32[]{:T(128)}) while((s32[]{:T(128)}, f32[128,128]{1,0:T(8,128)S(1)}, pred[]{:T(512)}, f32[128,128]{1,0:T(8,128)S(1)}, s32[]{:T(128)}) %tuple.93), condition=%wide.region_11.12_spmd.clone, body=%wide.region_10.11_spmd.clone.sunk | while | flops 25214976 | bytes 589926 | solution.py:89
  634.9 4.4 collective-permute-start
  639.4 4.3 collective-permute-done
  645.8 4.9 collective-permute-done
  652.9 4.9 collective-permute-done
  659.9 4.9 collective-permute-done
  666.9 4.9 collective-permute-done
  674.0 4.9 collective-permute-done
  681.0 4.9 collective-permute-done
  688.1 4.9 collective-permute-done
  695.1 4.9 collective-permute-done
  702.1 4.9 collective-permute-done
  709.2 4.9 collective-permute-done
  716.2 4.9 collective-permute-done
  723.2 4.9 collective-permute-done
  730.3 4.9 collective-permute-done
  737.3 4.9 collective-permute-done
  742.8 2.0 fusion.49
  (193 shorter events, 96.9 us)
Async XLA Ops:
  8.0 55.2 %all-gather.5.cloned.1.call-start = ((), (), s32[]{:S(2)}) async-start(), calls=%async_computation.1 | async-start | bytes 2228224 | tf_op jit(solution)/shard_map/while/body/eval_jaxpr/all_gather | solution.py:51
  72.2 53.5 %all-gather.5.cloned.1.call-start = ((), (), s32[]{:S(2)}) async-start(), calls=%async_computation.1 | async-start | bytes 2228224 | tf_op jit(solution)/shard_map/while/body/eval_jaxpr/all_gather | solution.py:51
  134.7 53.5 %all-gather.5.cloned.1.call-start = ((), (), s32[]{:S(2)}) async-start(), calls=%async_computation.1 | async-start | bytes 2228224 | tf_op jit(solution)/shard_map/while/body/eval_jaxpr/all_gather | solution.py:51
  197.2 53.2 %all-gather.5.cloned.1.call-start = ((), (), s32[]{:S(2)}) async-start(), calls=%async_computation.1 | async-start | bytes 2228224 | tf_op jit(solution)/shard_map/while/body/eval_jaxpr/all_gather | solution.py:51
  259.4 53.2 %all-gather.5.cloned.1.call-start = ((), (), s32[]{:S(2)}) async-start(), calls=%async_computation.1 | async-start | bytes 2228224 | tf_op jit(solution)/shard_map/while/body/eval_jaxpr/all_gather | solution.py:51
  321.6 53.2 %all-gather.5.cloned.1.call-start = ((), (), s32[]{:S(2)}) async-start(), calls=%async_computation.1 | async-start | bytes 2228224 | tf_op jit(solution)/shard_map/while/body/eval_jaxpr/all_gather | solution.py:51
  383.8 53.5 %all-gather.5.cloned.1.call-start = ((), (), s32[]{:S(2)}) async-start(), calls=%async_computation.1 | async-start | bytes 2228224 | tf_op jit(solution)/shard_map/while/body/eval_jaxpr/all_gather | solution.py:51
  446.3 53.5 %all-gather.5.cloned.1.call-start = ((), (), s32[]{:S(2)}) async-start(), calls=%async_computation.1 | async-start | bytes 2228224 | tf_op jit(solution)/shard_map/while/body/eval_jaxpr/all_gather | solution.py:51
  508.9 2.4 copy-start.6
  508.9 2.4 copy-start.7
  508.9 2.4 copy-start
  508.9 101.5 %all-reduce.2.cloned.1.call-start = ((), (), s32[]{:S(2)}) async-start(), calls=%async_computation | async-start | bytes 1048576 | tf_op jit(solution)/shard_map/psum | solution.py:67
  517.0 97.2 %copy-start.2 = (f32[128,128]{1,0:T(8,128)}, f32[128,128]{1,0:T(8,128)S(1)}, u32[]{:S(2)}) copy-start(f32[128,128]{1,0:T(8,128)S(1)} %fusion.29) | copy-start | bytes 196612
  610.4 3.8 copy-start.5
  626.9 3.2 copy-start.8
  627.6 3.0 copy-start.1
  630.4 2.3 copy-start.4
  630.6 4.1 copy-start.3
  634.9 8.8 %collective-permute-start = (f32[128,128]{1,0:T(8,128)S(1)}, f32[128,128]{1,0:T(8,128)S(1)}, u32[]{:S(2)}, u32[]{:S(2)}) collective-permute-start(f32[128,128]{1,0:T(8,128)S(1)} %fusion.120), channel_id=1, source_target_pairs={{16,0},{32,16},{48,32},{64,48},{80,64},{96,80},{112,96},{128,112},... | collective-permute-start | bytes 196616 | tf_op jit(solution)/shard_map/while/body/eval_jaxpr/ppermute | solution.py:13
  643.9 6.8 collective-permute-start
  650.9 6.8 collective-permute-start
  658.0 6.8 collective-permute-start
  665.0 6.8 collective-permute-start
  672.1 6.8 collective-permute-start
  679.1 6.8 collective-permute-start
  686.1 6.8 collective-permute-start
  693.2 6.8 collective-permute-start
  700.2 6.8 collective-permute-start
  707.2 6.8 collective-permute-start
  714.3 6.8 collective-permute-start
  721.3 6.8 collective-permute-start
  728.4 6.8 collective-permute-start
  735.4 6.8 collective-permute-start
Sparse Core Ops, SparseCore 0:
  12.2 50.9 all-gather.4
  76.3 49.3 all-gather.4
  138.8 49.3 all-gather.4
  201.0 49.3 all-gather.4
  263.2 49.3 all-gather.4
  325.4 49.3 all-gather.4
  387.9 49.3 all-gather.4
  450.5 49.3 all-gather.4
Sparse Core Ops, SparseCore 1:
  517.0 93.3 all-reduce.1
where the time goes:
time: 753 us; the launch traced here: 752 us
  waiting for transfers between devices  542 us (72%)
  matrix products  69.3 us (9%)
  local copies, waits for them, and re-layouts  51.2 us (7%)
  starting transfers between devices  31.4 us (4%)
  blocking collectives  31.1 us (4%)
  between operations  15.9 us (2%)
  other arithmetic  10 us (1%)
    all_gather x8, waiting for transfers between devices, observe_single_time(): whole = lax.all_gather(ensemble_shard, 'row', axis=1, tiled=True)  409 us
    ppermute x15, waiting for transfers between devices, passed_along(): return lax.ppermute(shard, axis, pairs)  72.4 us
    psum x1, waiting for transfers between devices, local(): info_matrix, info_vector = lax.psum((part_matrix, part_vector), 'row')  60.8 us
    dot_general x8, matrix products, observe_single_time(): jnp.einsum('mbkj,bkij->mbi', picked, nonzero_tiles, precision=exact_product)  34.8 us
    ppermute x15, starting transfers between devices, passed_along(): return lax.ppermute(shard, axis, pairs)  31.3 us
    psum x1, blocking collectives, local(): info_matrix, info_vector = lax.psum((part_matrix, part_vector), 'row')  31.1 us
    gather x8, local copies, waits for them, and re-layouts, observe_single_time(): whole.reshape(ensemble_entries, column_count, block_size)  15.9 us
    reshape x8, local copies, waits for them, and re-layouts, observe_single_time(): whole.reshape(ensemble_entries, column_count, block_size)  15.3 us
  transfers between devices with their start and end apart: 24, of which 24 were waited for; matrix products, arithmetic and copies ran while one was open for 1% of the time, Pallas kernels for 0%

commit v1 on v0

--- a/solution.py
+++ b/solution.py
@@ -48,7 +48,9 @@
     local_rows = nonzero_tiles.shape[0] * block_size
 
     def observe_single_time(ensemble_shard):
-        whole = lax.all_gather(ensemble_shard, "row", axis=1, tiled=True)
+        whole = jnp.concatenate(
+            lax.all_to_all(jnp.stack([ensemble_shard] * lax.axis_size("row")), "row", 0, 0), axis=1
+        )
         column_count = whole.shape[1] // block_size
         picked = whole.reshape(ensemble_entries, column_count, block_size)[:, nonzero_tile_targets]
         result = jnp.einsum("mbkj,bkij->mbi", picked, nonzero_tiles, precision=exact_product)

time: 753 us -> 602 us (0.80)
  waiting for transfers between devices: 542 us -> 340 us
  starting transfers between devices: 31.4 us -> 84 us
  local copies, waits for them, and re-layouts: 51.2 us -> 59.5 us
    all_gather x8 -> x0, waiting for transfers between devices: 409 us -> none  [observe_single_time(): whole = lax.all_gather(ensemble_shard, 'row', axis=1, tiled=True)]
    all_to_all x0 -> x8, waiting for transfers between devices: none -> 203 us  [observe_single_time(): lax.all_to_all(jnp.stack([ensemble_shard] * lax.axis_size('row')), 'row',...]
    all_to_all x0 -> x8, starting transfers between devices: none -> 53.2 us  [observe_single_time(): lax.all_to_all(jnp.stack([ensemble_shard] * lax.axis_size('row')), 'row',...]
    another operation x0 -> x8, local copies, waits for them, and re-layouts: none -> 12.2 us  [observe_single_time(): jnp.stack([ensemble_shard] * lax.axis_size('row'))]
  transfers between devices with their start and end apart: 24 -> 24, of which waited for: 24 -> 24; matrix products, arithmetic and copies ran while one was open for 1% -> 0% of each run, Pallas kernels for 0% -> 0%
where the time goes in v1:
time: 602 us; the launch traced here: 600 us
  waiting for transfers between devices  340 us (56%)
  starting transfers between devices  84 us (14%)
  matrix products  64.3 us (11%)
  local copies, waits for them, and re-layouts  59.5 us (10%)
  blocking collectives  32.5 us (5%)
  between operations  14.4 us (2%)
    all_to_all x8, waiting for transfers between devices, observe_single_time(): lax.all_to_all(jnp.stack([ensemble_shard] * lax.axis_size('row')), 'row',...  203 us
    ppermute x15, waiting for transfers between devices, passed_along(): return lax.ppermute(shard, axis, pairs)  72.4 us
    psum x1, waiting for transfers between devices, local(): info_matrix, info_vector = lax.psum((part_matrix, part_vector), 'row')  64.5 us
    all_to_all x8, starting transfers between devices, observe_single_time(): lax.all_to_all(jnp.stack([ensemble_shard] * lax.axis_size('row')), 'row',...  53.2 us
    psum x1, blocking collectives, local(): info_matrix, info_vector = lax.psum((part_matrix, part_vector), 'row')  32.5 us
    ppermute x15, starting transfers between devices, passed_along(): return lax.ppermute(shard, axis, pairs)  30.8 us
    dot_general x8, matrix products, observe_single_time(): jnp.einsum('mbkj,bkij->mbi', picked, nonzero_tiles, precision=exact_product)  29.8 us
    gather x8, local copies, waits for them, and re-layouts, observe_single_time(): whole.reshape(ensemble_entries, column_count, block_size)  18.2 us
  transfers between devices with their start and end apart: 24, of which 24 were waited for; matrix products, arithmetic and copies ran while one was open for 0% of the time, Pallas kernels for 0%

profile of v1, /device:TPU:97, one launch (start us, length us, event | category | flops | bytes accessed | tf_op | source)
XLA Modules:
  0.0 600.4 jit_solution(1152252167133277179)
XLA Ops:
  7.2 345.9 %while.39 = (s32[]{:T(128)}, f32[8,128,512]{1,2,0:T(8,128)}, f32[8,128,256]{2,1,0:T(8,128)}, s32[4,8]{1,0:T(4,128)}, f32[4,8,128,128]{3,2,1,0:T(8,128)}, /*index=5*/s32[]{:T(128)}) while((s32[]{:T(128)}, f32[8,128,512]{1,2,0:T(8,128)}, f32[8,128,256]{2,1,0:T(8,128)}, s32[4,8]{1,0:T(4,128)}, f32[4,8,128,128]{3,2,1,0:T(8,128)}, ...), condition=%wide.region_1.2_spmd, body=%wide.region_0.1_spmd.sunk | while | flops 805307520 | bytes 22418832 | solution.py:59
  9.8 6.9 %all-to-all-start = ((f32[16,128,256]{1,2,0:T(8,128)}), f32[16,128,256]{1,2,0:T(8,128)S(1)}, u32[]{:S(2)}, u32[]{:S(2)}) async-start(f32[16,128,256]{1,2,0:T(8,128)} %stack.3), calls=%async_computation | async-start | bytes 4194304 | tf_op jit(solution)/shard_map/while/body/eval_jaxpr/all_to_all | solution.py:52
  16.8 27.8 %all-to-all-done = f32[16,128,256]{1,2,0:T(8,128)S(1)} async-done(((f32[16,128,256]{1,2,0:T(8,128)}), f32[16,128,256]{1,2,0:T(8,128)S(1)}, u32[]{:S(2)}, u32[]{:S(2)}) %all-to-all-start) | async-done | bytes 2097184 | tf_op jit(solution)/shard_map/while/body/eval_jaxpr/all_to_all | solution.py:52
  46.4 2.3 gather_fusion
  48.6 3.7 fusion.116
  55.6 4.0 all-to-all-start
  59.8 25.1 %all-to-all-done = f32[16,128,256]{1,2,0:T(8,128)S(1)} async-done(((f32[16,128,256]{1,2,0:T(8,128)}), f32[16,128,256]{1,2,0:T(8,128)S(1)}, u32[]{:S(2)}, u32[]{:S(2)}) %all-to-all-start) | async-done | bytes 2097184 | tf_op jit(solution)/shard_map/while/body/eval_jaxpr/all_to_all | solution.py:52
  86.7 2.3 gather_fusion
  89.0 3.7 fusion.116
  96.0 6.9 %all-to-all-start = ((f32[16,128,256]{1,2,0:T(8,128)}), f32[16,128,256]{1,2,0:T(8,128)S(1)}, u32[]{:S(2)}, u32[]{:S(2)}) async-start(f32[16,128,256]{1,2,0:T(8,128)} %stack.3), calls=%async_computation | async-start | bytes 4194304 | tf_op jit(solution)/shard_map/while/body/eval_jaxpr/all_to_all | solution.py:52
  103.0 25.0 %all-to-all-done = f32[16,128,256]{1,2,0:T(8,128)S(1)} async-done(((f32[16,128,256]{1,2,0:T(8,128)}), f32[16,128,256]{1,2,0:T(8,128)S(1)}, u32[]{:S(2)}, u32[]{:S(2)}) %all-to-all-start) | async-done | bytes 2097184 | tf_op jit(solution)/shard_map/while/body/eval_jaxpr/all_to_all | solution.py:52
  132.0 3.7 fusion.116
  139.0 7.1 %all-to-all-start = ((f32[16,128,256]{1,2,0:T(8,128)}), f32[16,128,256]{1,2,0:T(8,128)S(1)}, u32[]{:S(2)}, u32[]{:S(2)}) async-start(f32[16,128,256]{1,2,0:T(8,128)} %stack.3), calls=%async_computation | async-start | bytes 4194304 | tf_op jit(solution)/shard_map/while/body/eval_jaxpr/all_to_all | solution.py:52
  146.3 25.0 %all-to-all-done = f32[16,128,256]{1,2,0:T(8,128)S(1)} async-done(((f32[16,128,256]{1,2,0:T(8,128)}), f32[16,128,256]{1,2,0:T(8,128)S(1)}, u32[]{:S(2)}, u32[]{:S(2)}) %all-to-all-start) | async-done | bytes 2097184 | tf_op jit(solution)/shard_map/while/body/eval_jaxpr/all_to_all | solution.py:52
  175.4 3.7 fusion.116
  182.4 7.1 %all-to-all-start = ((f32[16,128,256]{1,2,0:T(8,128)}), f32[16,128,256]{1,2,0:T(8,128)S(1)}, u32[]{:S(2)}, u32[]{:S(2)}) async-start(f32[16,128,256]{1,2,0:T(8,128)} %stack.3), calls=%async_computation | async-start | bytes 4194304 | tf_op jit(solution)/shard_map/while/body/eval_jaxpr/all_to_all | solution.py:52
  189.6 25.1 %all-to-all-done = f32[16,128,256]{1,2,0:T(8,128)S(1)} async-done(((f32[16,128,256]{1,2,0:T(8,128)}), f32[16,128,256]{1,2,0:T(8,128)S(1)}, u32[]{:S(2)}, u32[]{:S(2)}) %all-to-all-start) | async-done | bytes 2097184 | tf_op jit(solution)/shard_map/while/body/eval_jaxpr/all_to_all | solution.py:52
  218.8 3.7 fusion.116
  225.8 6.9 %all-to-all-start = ((f32[16,128,256]{1,2,0:T(8,128)}), f32[16,128,256]{1,2,0:T(8,128)S(1)}, u32[]{:S(2)}, u32[]{:S(2)}) async-start(f32[16,128,256]{1,2,0:T(8,128)} %stack.3), calls=%async_computation | async-start | bytes 4194304 | tf_op jit(solution)/shard_map/while/body/eval_jaxpr/all_to_all | solution.py:52
  232.8 25.0 %all-to-all-done = f32[16,128,256]{1,2,0:T(8,128)S(1)} async-done(((f32[16,128,256]{1,2,0:T(8,128)}), f32[16,128,256]{1,2,0:T(8,128)S(1)}, u32[]{:S(2)}, u32[]{:S(2)}) %all-to-all-start) | async-done | bytes 2097184 | tf_op jit(solution)/shard_map/while/body/eval_jaxpr/all_to_all | solution.py:52
  261.9 3.7 fusion.116
  268.9 7.1 %all-to-all-start = ((f32[16,128,256]{1,2,0:T(8,128)}), f32[16,128,256]{1,2,0:T(8,128)S(1)}, u32[]{:S(2)}, u32[]{:S(2)}) async-start(f32[16,128,256]{1,2,0:T(8,128)} %stack.3), calls=%async_computation | async-start | bytes 4194304 | tf_op jit(solution)/shard_map/while/body/eval_jaxpr/all_to_all | solution.py:52
  276.1 25.0 %all-to-all-done = f32[16,128,256]{1,2,0:T(8,128)S(1)} async-done(((f32[16,128,256]{1,2,0:T(8,128)}), f32[16,128,256]{1,2,0:T(8,128)S(1)}, u32[]{:S(2)}, u32[]{:S(2)}) %all-to-all-start) | async-done | bytes 2097184 | tf_op jit(solution)/shard_map/while/body/eval_jaxpr/all_to_all | solution.py:52
  305.2 3.7 fusion.116
  312.3 7.1 %all-to-all-start = ((f32[16,128,256]{1,2,0:T(8,128)}), f32[16,128,256]{1,2,0:T(8,128)S(1)}, u32[]{:S(2)}, u32[]{:S(2)}) async-start(f32[16,128,256]{1,2,0:T(8,128)} %stack.3), calls=%async_computation | async-start | bytes 4194304 | tf_op jit(solution)/shard_map/while/body/eval_jaxpr/all_to_all | solution.py:52
  319.5 25.1 %all-to-all-done = f32[16,128,256]{1,2,0:T(8,128)S(1)} async-done(((f32[16,128,256]{1,2,0:T(8,128)}), f32[16,128,256]{1,2,0:T(8,128)S(1)}, u32[]{:S(2)}, u32[]{:S(2)}) %all-to-all-start) | async-done | bytes 2097184 | tf_op jit(solution)/shard_map/while/body/eval_jaxpr/all_to_all | solution.py:52
  348.6 3.7 fusion.116
  353.1 2.4 reduce_sum.27
  355.5 5.6 fusion.7
  362.7 32.5 %psum.15 = f32[8,128]{1,0:T(8,128)S(1)} all-reduce(f32[8,128]{1,0:T(8,128)S(1)} %bitcast.129), channel_id=1, replica_groups=mesh['tm'=16,'row'=16] {'row'}, use_global_device_ids=true, to_apply=%region_6.7 | all-reduce | flops 1024 | bytes 8192 | tf_op jit(solution)/shard_map/psum | solution.py:69
  395.2 64.5 %all-reduce.2.cloned.1.call-done = f32[8,128,128]{2,1,0:T(8,128)} async-done(((f32[8,128,128]{2,1,0:T(8,128)}), f32[8,128,128]{2,1,0:T(8,128)}) %all-reduce.2.cloned.1.call-update) | async-done | bytes 524304 | tf_op jit(solution)/shard_map/psum | solution.py:69
  483.9 107.0 %while.41 = (s32[]{:T(128)}, f32[128,128]{1,0:T(8,128)S(1)}, pred[]{:T(512)}, f32[128,128]{1,0:T(8,128)S(1)}, s32[]{:T(128)}) while((s32[]{:T(128)}, f32[128,128]{1,0:T(8,128)S(1)}, pred[]{:T(512)}, f32[128,128]{1,0:T(8,128)S(1)}, s32[]{:T(128)}) %tuple.91), condition=%wide.region_11.12_spmd.clone, body=%wide.region_10.11_spmd.clone.sunk | while | flops 25214976 | bytes 589926 | solution.py:91
  484.2 3.9 collective-permute-start
  488.1 4.3 collective-permute-done
  494.5 4.9 collective-permute-done
  501.6 4.9 collective-permute-done
  508.6 4.9 collective-permute-done
  515.6 4.9 collective-permute-done
  522.7 4.9 collective-permute-done
  529.7 4.9 collective-permute-done
  536.8 4.9 collective-permute-done
  543.8 4.9 collective-permute-done
  550.8 4.9 collective-permute-done
  557.9 4.9 collective-permute-done
  564.9 4.9 collective-permute-done
  571.9 4.9 collective-permute-done
  579.0 4.9 collective-permute-done
  586.0 4.9 collective-permute-done
  (209 shorter events, 115.0 us)
Async XLA Ops:
  7.2 452.5 %all-reduce.2.cloned.1.call-start = ((), (), s32[]{:S(2)}) async-start(), calls=%async_computation.1 | async-start | bytes 1048576 | tf_op jit(solution)/shard_map/psum | solution.py:69
  9.8 6.9 %copy-start.6 = (s32[4,8]{1,0:T(4,128)S(1)}, s32[4,8]{1,0:T(4,128)}, u32[]{:S(2)}) copy-start(s32[4,8]{1,0:T(4,128)} %get-tuple-element.327) | copy-start | bytes 388 | tf_op jit(solution)/shard_map/while
  9.8 34.8 %all-to-all-start = ((f32[16,128,256]{1,2,0:T(8,128)}), f32[16,128,256]{1,2,0:T(8,128)S(1)}, u32[]{:S(2)}, u32[]{:S(2)}) async-start(f32[16,128,256]{1,2,0:T(8,128)} %stack.3), calls=%async_computation | async-start | bytes 4194304 | tf_op jit(solution)/shard_map/while/body/eval_jaxpr/all_to_all | solution.py:52
  55.6 4.1 copy-start.6
  55.6 29.2 %all-to-all-start = ((f32[16,128,256]{1,2,0:T(8,128)}), f32[16,128,256]{1,2,0:T(8,128)S(1)}, u32[]{:S(2)}, u32[]{:S(2)}) async-start(f32[16,128,256]{1,2,0:T(8,128)} %stack.3), calls=%async_computation | async-start | bytes 4194304 | tf_op jit(solution)/shard_map/while/body/eval_jaxpr/all_to_all | solution.py:52
  96.0 6.9 %copy-start.6 = (s32[4,8]{1,0:T(4,128)S(1)}, s32[4,8]{1,0:T(4,128)}, u32[]{:S(2)}) copy-start(s32[4,8]{1,0:T(4,128)} %get-tuple-element.327) | copy-start | bytes 388 | tf_op jit(solution)/shard_map/while
  96.0 32.0 %all-to-all-start = ((f32[16,128,256]{1,2,0:T(8,128)}), f32[16,128,256]{1,2,0:T(8,128)S(1)}, u32[]{:S(2)}, u32[]{:S(2)}) async-start(f32[16,128,256]{1,2,0:T(8,128)} %stack.3), calls=%async_computation | async-start | bytes 4194304 | tf_op jit(solution)/shard_map/while/body/eval_jaxpr/all_to_all | solution.py:52
  139.0 7.1 %copy-start.6 = (s32[4,8]{1,0:T(4,128)S(1)}, s32[4,8]{1,0:T(4,128)}, u32[]{:S(2)}) copy-start(s32[4,8]{1,0:T(4,128)} %get-tuple-element.327) | copy-start | bytes 388 | tf_op jit(solution)/shard_map/while
  139.0 32.2 %all-to-all-start = ((f32[16,128,256]{1,2,0:T(8,128)}), f32[16,128,256]{1,2,0:T(8,128)S(1)}, u32[]{:S(2)}, u32[]{:S(2)}) async-start(f32[16,128,256]{1,2,0:T(8,128)} %stack.3), calls=%async_computation | async-start | bytes 4194304 | tf_op jit(solution)/shard_map/while/body/eval_jaxpr/all_to_all | solution.py:52
  182.4 7.1 %copy-start.6 = (s32[4,8]{1,0:T(4,128)S(1)}, s32[4,8]{1,0:T(4,128)}, u32[]{:S(2)}) copy-start(s32[4,8]{1,0:T(4,128)} %get-tuple-element.327) | copy-start | bytes 388 | tf_op jit(solution)/shard_map/while
  182.4 32.3 %all-to-all-start = ((f32[16,128,256]{1,2,0:T(8,128)}), f32[16,128,256]{1,2,0:T(8,128)S(1)}, u32[]{:S(2)}, u32[]{:S(2)}) async-start(f32[16,128,256]{1,2,0:T(8,128)} %stack.3), calls=%async_computation | async-start | bytes 4194304 | tf_op jit(solution)/shard_map/while/body/eval_jaxpr/all_to_all | solution.py:52
  225.8 6.9 %copy-start.6 = (s32[4,8]{1,0:T(4,128)S(1)}, s32[4,8]{1,0:T(4,128)}, u32[]{:S(2)}) copy-start(s32[4,8]{1,0:T(4,128)} %get-tuple-element.327) | copy-start | bytes 388 | tf_op jit(solution)/shard_map/while
  225.8 32.0 %all-to-all-start = ((f32[16,128,256]{1,2,0:T(8,128)}), f32[16,128,256]{1,2,0:T(8,128)S(1)}, u32[]{:S(2)}, u32[]{:S(2)}) async-start(f32[16,128,256]{1,2,0:T(8,128)} %stack.3), calls=%async_computation | async-start | bytes 4194304 | tf_op jit(solution)/shard_map/while/body/eval_jaxpr/all_to_all | solution.py:52
  268.9 7.1 %copy-start.6 = (s32[4,8]{1,0:T(4,128)S(1)}, s32[4,8]{1,0:T(4,128)}, u32[]{:S(2)}) copy-start(s32[4,8]{1,0:T(4,128)} %get-tuple-element.327) | copy-start | bytes 388 | tf_op jit(solution)/shard_map/while
  268.9 32.2 %all-to-all-start = ((f32[16,128,256]{1,2,0:T(8,128)}), f32[16,128,256]{1,2,0:T(8,128)S(1)}, u32[]{:S(2)}, u32[]{:S(2)}) async-start(f32[16,128,256]{1,2,0:T(8,128)} %stack.3), calls=%async_computation | async-start | bytes 4194304 | tf_op jit(solution)/shard_map/while/body/eval_jaxpr/all_to_all | solution.py:52
  312.2 7.1 %copy-start.6 = (s32[4,8]{1,0:T(4,128)S(1)}, s32[4,8]{1,0:T(4,128)}, u32[]{:S(2)}) copy-start(s32[4,8]{1,0:T(4,128)} %get-tuple-element.327) | copy-start | bytes 388 | tf_op jit(solution)/shard_map/while
  312.3 32.3 %all-to-all-start = ((f32[16,128,256]{1,2,0:T(8,128)}), f32[16,128,256]{1,2,0:T(8,128)S(1)}, u32[]{:S(2)}, u32[]{:S(2)}) async-start(f32[16,128,256]{1,2,0:T(8,128)} %stack.3), calls=%async_computation | async-start | bytes 4194304 | tf_op jit(solution)/shard_map/while/body/eval_jaxpr/all_to_all | solution.py:52
  353.1 2.4 copy-start.7
  353.1 2.4 copy-start.8
  353.1 2.4 copy-start
  361.2 102.3 %copy-start.2 = (f32[128,128]{1,0:T(8,128)}, f32[128,128]{1,0:T(8,128)S(1)}, u32[]{:S(2)}) copy-start(f32[128,128]{1,0:T(8,128)S(1)} %fusion.29) | copy-start | bytes 196612
  459.7 3.8 copy-start.5
  476.2 3.2 copy-start.9
  476.8 3.0 copy-start.1
  479.6 2.3 copy-start.4
  479.9 4.1 copy-start.3
  484.2 8.2 %collective-permute-start = (f32[128,128]{1,0:T(8,128)S(1)}, f32[128,128]{1,0:T(8,128)S(1)}, u32[]{:S(2)}, u32[]{:S(2)}) collective-permute-start(f32[128,128]{1,0:T(8,128)S(1)} %fusion.120), channel_id=1, source_target_pairs={{16,0},{32,16},{48,32},{64,48},{80,64},{96,80},{112,96},{128,112},... | collective-permute-start | bytes 196616 | tf_op jit(solution)/shard_map/while/body/eval_jaxpr/ppermute | solution.py:13
  492.6 6.8 %collective-permute-start = (f32[128,128]{1,0:T(8,128)S(1)}, f32[128,128]{1,0:T(8,128)S(1)}, u32[]{:S(2)}, u32[]{:S(2)}) collective-permute-start(f32[128,128]{1,0:T(8,128)S(1)} %fusion.120), channel_id=1, source_target_pairs={{16,0},{32,16},{48,32},{64,48},{80,64},{96,80},{112,96},{128,112},... | collective-permute-start | bytes 196616 | tf_op jit(solution)/shard_map/while/body/eval_jaxpr/ppermute | solution.py:13
  499.6 6.8 %collective-permute-start = (f32[128,128]{1,0:T(8,128)S(1)}, f32[128,128]{1,0:T(8,128)S(1)}, u32[]{:S(2)}, u32[]{:S(2)}) collective-permute-start(f32[128,128]{1,0:T(8,128)S(1)} %fusion.120), channel_id=1, source_target_pairs={{16,0},{32,16},{48,32},{64,48},{80,64},{96,80},{112,96},{128,112},... | collective-permute-start | bytes 196616 | tf_op jit(solution)/shard_map/while/body/eval_jaxpr/ppermute | solution.py:13
  506.7 6.8 %collective-permute-start = (f32[128,128]{1,0:T(8,128)S(1)}, f32[128,128]{1,0:T(8,128)S(1)}, u32[]{:S(2)}, u32[]{:S(2)}) collective-permute-start(f32[128,128]{1,0:T(8,128)S(1)} %fusion.120), channel_id=1, source_target_pairs={{16,0},{32,16},{48,32},{64,48},{80,64},{96,80},{112,96},{128,112},... | collective-permute-start | bytes 196616 | tf_op jit(solution)/shard_map/while/body/eval_jaxpr/ppermute | solution.py:13
  513.7 6.8 %collective-permute-start = (f32[128,128]{1,0:T(8,128)S(1)}, f32[128,128]{1,0:T(8,128)S(1)}, u32[]{:S(2)}, u32[]{:S(2)}) collective-permute-start(f32[128,128]{1,0:T(8,128)S(1)} %fusion.120), channel_id=1, source_target_pairs={{16,0},{32,16},{48,32},{64,48},{80,64},{96,80},{112,96},{128,112},... | collective-permute-start | bytes 196616 | tf_op jit(solution)/shard_map/while/body/eval_jaxpr/ppermute | solution.py:13
  520.8 6.8 %collective-permute-start = (f32[128,128]{1,0:T(8,128)S(1)}, f32[128,128]{1,0:T(8,128)S(1)}, u32[]{:S(2)}, u32[]{:S(2)}) collective-permute-start(f32[128,128]{1,0:T(8,128)S(1)} %fusion.120), channel_id=1, source_target_pairs={{16,0},{32,16},{48,32},{64,48},{80,64},{96,80},{112,96},{128,112},... | collective-permute-start | bytes 196616 | tf_op jit(solution)/shard_map/while/body/eval_jaxpr/ppermute | solution.py:13
  527.8 6.8 %collective-permute-start = (f32[128,128]{1,0:T(8,128)S(1)}, f32[128,128]{1,0:T(8,128)S(1)}, u32[]{:S(2)}, u32[]{:S(2)}) collective-permute-start(f32[128,128]{1,0:T(8,128)S(1)} %fusion.120), channel_id=1, source_target_pairs={{16,0},{32,16},{48,32},{64,48},{80,64},{96,80},{112,96},{128,112},... | collective-permute-start | bytes 196616 | tf_op jit(solution)/shard_map/while/body/eval_jaxpr/ppermute | solution.py:13
  534.8 6.8 %collective-permute-start = (f32[128,128]{1,0:T(8,128)S(1)}, f32[128,128]{1,0:T(8,128)S(1)}, u32[]{:S(2)}, u32[]{:S(2)}) collective-permute-start(f32[128,128]{1,0:T(8,128)S(1)} %fusion.120), channel_id=1, source_target_pairs={{16,0},{32,16},{48,32},{64,48},{80,64},{96,80},{112,96},{128,112},... | collective-permute-start | bytes 196616 | tf_op jit(solution)/shard_map/while/body/eval_jaxpr/ppermute | solution.py:13
  541.9 6.8 %collective-permute-start = (f32[128,128]{1,0:T(8,128)S(1)}, f32[128,128]{1,0:T(8,128)S(1)}, u32[]{:S(2)}, u32[]{:S(2)}) collective-permute-start(f32[128,128]{1,0:T(8,128)S(1)} %fusion.120), channel_id=1, source_target_pairs={{16,0},{32,16},{48,32},{64,48},{80,64},{96,80},{112,96},{128,112},... | collective-permute-start | bytes 196616 | tf_op jit(solution)/shard_map/while/body/eval_jaxpr/ppermute | solution.py:13
  548.9 6.8 %collective-permute-start = (f32[128,128]{1,0:T(8,128)S(1)}, f32[128,128]{1,0:T(8,128)S(1)}, u32[]{:S(2)}, u32[]{:S(2)}) collective-permute-start(f32[128,128]{1,0:T(8,128)S(1)} %fusion.120), channel_id=1, source_target_pairs={{16,0},{32,16},{48,32},{64,48},{80,64},{96,80},{112,96},{128,112},... | collective-permute-start | bytes 196616 | tf_op jit(solution)/shard_map/while/body/eval_jaxpr/ppermute | solution.py:13
  555.9 6.8 %collective-permute-start = (f32[128,128]{1,0:T(8,128)S(1)}, f32[128,128]{1,0:T(8,128)S(1)}, u32[]{:S(2)}, u32[]{:S(2)}) collective-permute-start(f32[128,128]{1,0:T(8,128)S(1)} %fusion.120), channel_id=1, source_target_pairs={{16,0},{32,16},{48,32},{64,48},{80,64},{96,80},{112,96},{128,112},... | collective-permute-start | bytes 196616 | tf_op jit(solution)/shard_map/while/body/eval_jaxpr/ppermute | solution.py:13
  563.0 6.8 %collective-permute-start = (f32[128,128]{1,0:T(8,128)S(1)}, f32[128,128]{1,0:T(8,128)S(1)}, u32[]{:S(2)}, u32[]{:S(2)}) collective-permute-start(f32[128,128]{1,0:T(8,128)S(1)} %fusion.120), channel_id=1, source_target_pairs={{16,0},{32,16},{48,32},{64,48},{80,64},{96,80},{112,96},{128,112},... | collective-permute-start | bytes 196616 | tf_op jit(solution)/shard_map/while/body/eval_jaxpr/ppermute | solution.py:13
  570.0 6.8 %collective-permute-start = (f32[128,128]{1,0:T(8,128)S(1)}, f32[128,128]{1,0:T(8,128)S(1)}, u32[]{:S(2)}, u32[]{:S(2)}) collective-permute-start(f32[128,128]{1,0:T(8,128)S(1)} %fusion.120), channel_id=1, source_target_pairs={{16,0},{32,16},{48,32},{64,48},{80,64},{96,80},{112,96},{128,112},... | collective-permute-start | bytes 196616 | tf_op jit(solution)/shard_map/while/body/eval_jaxpr/ppermute | solution.py:13
  577.1 6.8 %collective-permute-start = (f32[128,128]{1,0:T(8,128)S(1)}, f32[128,128]{1,0:T(8,128)S(1)}, u32[]{:S(2)}, u32[]{:S(2)}) collective-permute-start(f32[128,128]{1,0:T(8,128)S(1)} %fusion.120), channel_id=1, source_target_pairs={{16,0},{32,16},{48,32},{64,48},{80,64},{96,80},{112,96},{128,112},... | collective-permute-start | bytes 196616 | tf_op jit(solution)/shard_map/while/body/eval_jaxpr/ppermute | solution.py:13
  584.1 6.8 %collective-permute-start = (f32[128,128]{1,0:T(8,128)S(1)}, f32[128,128]{1,0:T(8,128)S(1)}, u32[]{:S(2)}, u32[]{:S(2)}) collective-permute-start(f32[128,128]{1,0:T(8,128)S(1)} %fusion.120), channel_id=1, source_target_pairs={{16,0},{32,16},{48,32},{64,48},{80,64},{96,80},{112,96},{128,112},... | collective-permute-start | bytes 196616 | tf_op jit(solution)/shard_map/while/body/eval_jaxpr/ppermute | solution.py:13
Sparse Core Ops, SparseCore 0:
  361.3 98.3 all-reduce.1
